TPU v7x, 128 devices: a whole 4x4x4 slice. The times are simulated.
128 devices in a mesh: row: 8 (over z, core), col: 16 (over y, x).
Axes of the slice: x: 4, y: 4, z: 4, core: 2. Of those that a mesh axis runs over, the one named last changes fastest.
Arguments:
- singles: bfloat16 [1024, 384], P('row', 'col'), may hold values from -6 to 6
- pair_in: bfloat16 [1024, 1024, 128], P('row', 'col'), may hold values from -6 to 6
- proj_weight: bfloat16 [384, 256], P('col'), may hold values from -0.3125 to 0.3125
- gain_first: float32 [128], replicated, may hold values from 0.1 to 1.9
- first_in: bfloat16 [128, 1024], replicated, may hold values from -0.5 to 0.5
- first_out: bfloat16 [512, 128], replicated, may hold values from -0.25 to 0.25
- gain_second: float32 [128], replicated, may hold values from 0.1 to 1.9
- second_in: bfloat16 [128, 1024], replicated, may hold values from -0.5 to 0.5
- second_out: bfloat16 [512, 128], replicated, may hold values from -0.25 to 0.25
- head_weight: bfloat16 [128, 64], replicated, may hold values from -1.5 to 1.5
- pae_bins: int32 [1024, 1024], P('row', 'col'), may hold values from 0 to 63
- chain_perm: int32 [1024], replicated, may hold values from 0 to 1023, as said below
- resolved_counts: int32 [8, 16], P('row'), may hold values from 1 to 256, 2048 in all within a row
- tile_order: int32 [8, 4096], P('row', 'col'), may hold values from 0 to 255, as said below
Outputs:
- pair_grad: bfloat16 [1024, 1024, 128], P('row', 'col')
- single_grad: float32 [1024, 384], P('row', 'col')
- second_in_grad: float32 [128, 1024], replicated
- second_out_grad: float32 [512, 128], replicated
- head_grad: float32 [128, 64], replicated
Inputs may be any that keep to these rules, and one draw needn't show every extreme that they name: chain_perm maps every aligned group of 64 tokens onto itself, moving whole aligned runs of 16 tokens and keeping the order inside a run. Each row of resolved_counts sums to 2048, and its largest entry is 256. In each row of tile_order, entries b * 256 to (b + 1) * 256 - 1 are a permutation of 0 to 255.
All inputs are finite; a program needn't handle non-finite values.
Results may differ from a plain program's by a relative error of at most 0.011.
Values may be sent and summed in bfloat16 or wider, within the bound.
A program may use at most 64 MiB of HBM per device.

v0:
```python
import jax
import jax.numpy as jnp
from jax import lax
from jax.sharding import PartitionSpec as P

TILE = 32


def contract(left_op, right_op, left_dim, right_dim):
    return lax.dot_general(
        left_op,
        right_op,
        (((left_dim,), (right_dim,)), ((), ())),
        preferred_element_type=jnp.float32,
    )


def block_size(extent, per_item, limit):
    best = 1
    for candidate in range(1, extent + 1):
        if extent % candidate == 0 and candidate * per_item <= limit:
            best = candidate
    return best


def transition_forward(start_z, gain_vec, w_in, w_out):
    hidden_units = w_out.shape[0]
    average = jnp.mean(start_z, axis=-1, keepdims=True)
    centred = start_z - average
    scaling = lax.rsqrt(jnp.mean(centred * centred, axis=-1, keepdims=True) + 1e-05)
    normed = centred * scaling
    inputs = (normed * gain_vec).astype(jnp.bfloat16)
    gate_up = jnp.dot(inputs, w_in, preferred_element_type=jnp.float32)
    gate_part = gate_up[:, :hidden_units]
    up_part = gate_up[:, hidden_units:]
    gate_sig = jax.nn.sigmoid(gate_part)
    hidden_act = (gate_part * gate_sig * up_part).astype(jnp.bfloat16)
    result = jnp.dot(hidden_act, w_out, preferred_element_type=jnp.float32)
    return (result, (normed, scaling, inputs, gate_part, up_part, gate_sig, hidden_act))


def transition_backward(saved, grad_out, gain_vec, w_in, w_out, with_weights):
    normed, scaling, inputs, gate_part, up_part, gate_sig, hidden_act = saved
    grad_hidden = contract(grad_out, w_out, 1, 1)
    grad_gate = grad_hidden * up_part * gate_sig * (1.0 + gate_part * (1.0 - gate_sig))
    grad_up = grad_hidden * gate_part * gate_sig
    grad_both = jnp.concatenate([grad_gate, grad_up], axis=1).astype(jnp.bfloat16)
    grad_normed = contract(grad_both, w_in, 1, 1) * gain_vec
    grad_field = scaling * (
        grad_normed
        - jnp.mean(grad_normed, axis=-1, keepdims=True)
        - normed * jnp.mean(grad_normed * normed, axis=-1, keepdims=True)
    )
    if with_weights:
        return (grad_field, contract(inputs, grad_both, 0, 0), contract(hidden_act, grad_out, 0, 0))
    return (grad_field, None, None)


def head_step(rounded_z, targets, keep_mask, head_weight):
    logits = jnp.dot(rounded_z, head_weight, preferred_element_type=jnp.float32)
    exponent = jnp.exp(logits - jnp.max(logits, axis=-1, keepdims=True))
    probability = exponent / jnp.sum(exponent, axis=-1, keepdims=True)
    onehot = (targets[:, None] == lax.broadcasted_iota(jnp.int32, logits.shape, 1)).astype(
        jnp.float32
    )
    grad_logits = ((probability - onehot) * keep_mask[:, None]).astype(jnp.bfloat16)
    return (
        contract(grad_logits, head_weight, 1, 1).astype(jnp.bfloat16),
        contract(rounded_z, grad_logits, 0, 0),
    )


def second_step(pair_one, targets, live_mask, gain_second, second_in, second_out, head_weight):
    start_f = pair_one.astype(jnp.float32)
    delta, saved = transition_forward(start_f, gain_second, second_in, second_out)
    rounded_z = (start_f + live_mask[:, None] * delta).astype(jnp.bfloat16)
    grad_two, head_part = head_step(rounded_z, targets, jnp.ones_like(live_mask), head_weight)
    masked_out = jnp.where(live_mask[:, None] > 0, grad_two, jnp.zeros((), jnp.bfloat16))
    back_field, in_part, out_part = transition_backward(
        saved, masked_out, gain_second, second_in, second_out, True
    )
    return (
        (grad_two.astype(jnp.float32) + back_field).astype(jnp.bfloat16),
        in_part,
        out_part,
        head_part,
    )


def local(
    singles,
    pair_in,
    proj_weight,
    gain_first,
    first_in,
    first_out,
    gain_second,
    second_in,
    second_out,
    head_weight,
    pae_bins,
    chain_perm,
    resolved_counts,
    tile_order,
):
    rows_dev, cols_dev, width = pair_in.shape
    tile_len = TILE
    tiles_dev = rows_dev * cols_dev // tile_len
    token_count = chain_perm.shape[0]
    row_index = lax.axis_index("row")
    col_index = lax.axis_index("col")
    col_count = lax.axis_size("col")
    partial_proj = jnp.dot(singles, proj_weight, preferred_element_type=jnp.float32)
    projected = lax.psum(partial_proj, "col")
    left_part = projected[:, :width]
    right_part = projected[:, width:].astype(jnp.bfloat16)
    col_start = col_index * cols_dev
    right_all = lax.all_gather(right_part, "row", axis=0, tiled=True)
    col_right = lax.dynamic_slice_in_dim(right_all, col_start, cols_dev, 0)
    col_right_f = col_right.astype(jnp.float32)
    block_rows = block_size(rows_dev, cols_dev, 1024)
    row_blocks = rows_dev // block_rows
    block_pairs = block_rows * cols_dev

    def start_field(block_index):
        first_row = block_index * block_rows
        pair_rows = lax.dynamic_slice_in_dim(pair_in, first_row, block_rows, 0).astype(jnp.float32)
        left_rows = lax.dynamic_slice_in_dim(left_part, first_row, block_rows, 0)
        field_rows = pair_rows + left_rows[:, None, :] + col_right_f[None, :, :]
        return field_rows.reshape(block_pairs, width)

    def forward_block(block_index):
        start_z = start_field(block_index)
        delta, unused_saved = transition_forward(start_z, gain_first, first_in, first_out)
        return (start_z + delta).astype(jnp.bfloat16)

    block_ids = jnp.arange(row_blocks, dtype=jnp.int32)
    pair_one = lax.map(forward_block, block_ids).reshape(rows_dev * cols_dev, width)
    live_count = resolved_counts[0, col_index]
    order_list = tile_order[0]
    tile_iota = jnp.arange(tiles_dev, dtype=jnp.int32)
    rank_of = jnp.sum(
        jnp.where(order_list[None, :] == tile_iota[:, None], tile_iota[None, :], 0), axis=1
    )
    tile_live = rank_of < live_count
    pair_live = jnp.repeat(tile_live, tile_len).astype(jnp.float32)
    perm_rows = (
        lax.dynamic_slice_in_dim(chain_perm, row_index * rows_dev, rows_dev, 0)
        - row_index * rows_dev
    )
    perm_cols = lax.dynamic_slice_in_dim(chain_perm, col_start, cols_dev, 0) - col_start
    targets = jnp.take(jnp.take(pae_bins, perm_rows, axis=0), perm_cols, axis=1).reshape(
        rows_dev * cols_dev
    )
    pair_stack = pair_one.reshape(row_blocks, block_pairs, width)
    target_stack = targets.reshape(row_blocks, block_pairs)
    live_stack = pair_live.reshape(row_blocks, block_pairs)
    zero_in = jnp.zeros(second_in.shape, jnp.float32)
    zero_out = jnp.zeros(second_out.shape, jnp.float32)
    zero_head = jnp.zeros(head_weight.shape, jnp.float32)

    def head_block(running, operands):
        grad_two, head_part = head_step(operands[0], operands[1], 1.0 - operands[2], head_weight)
        return (running + head_part, grad_two)

    head_sum, rest_stack = lax.scan(head_block, zero_head, (pair_stack, target_stack, live_stack))
    rest_tiles = rest_stack.reshape(tiles_dev, tile_len, width)
    slots = -(-tiles_dev // col_count)
    row_counts = resolved_counts[0]
    offsets = jnp.cumsum(row_counts) - row_counts
    my_offset = offsets[col_index]
    worker_iota = jnp.arange(col_count, dtype=jnp.int32)[:, None]
    slot_iota = jnp.arange(slots, dtype=jnp.int32)[None, :]
    send_rank = col_count * slot_iota + jnp.mod(worker_iota - my_offset, col_count)
    send_valid = send_rank < live_count
    send_ids = order_list[jnp.minimum(send_rank, tiles_dev - 1)]
    tile_view = pair_one.reshape(tiles_dev, tile_len, width)
    target_view = targets.reshape(tiles_dev, tile_len).astype(jnp.bfloat16)
    send_pairs = jnp.where(
        send_valid[:, :, None, None], tile_view[send_ids], jnp.zeros((), jnp.bfloat16)
    )
    send_targets = jnp.where(
        send_valid[:, :, None], target_view[send_ids], jnp.zeros((), jnp.bfloat16)
    )
    recv_pairs, recv_targets = (
        lax.all_to_all(send_pairs, "col", split_axis=0, concat_axis=0, tiled=True),
        lax.all_to_all(send_targets, "col", split_axis=0, concat_axis=0, tiled=True),
    )
    work_count = tiles_dev // 2
    position = jnp.arange(work_count, dtype=jnp.int32)
    global_rank = col_count * position + col_index
    source = jnp.sum((offsets[None, :] <= global_rank[:, None]).astype(jnp.int32), axis=1) - 1
    source_slot = (global_rank - offsets[source]) // col_count
    flat_index = source * slots + source_slot
    work_pairs = recv_pairs.reshape(col_count * slots, tile_len, width)[flat_index]
    work_targets = recv_targets.reshape(col_count * slots, tile_len)[flat_index].astype(jnp.int32)
    block_tiles = block_size(work_count, tile_len, 1024)
    work_blocks = work_count // block_tiles
    work_pair_stack = work_pairs.reshape(work_blocks, block_tiles * tile_len, width)
    work_target_stack = work_targets.reshape(work_blocks, block_tiles * tile_len)

    def worker_block(running, operands):
        all_live = jnp.ones(operands[1].shape, jnp.float32)
        grad_one, in_part, out_part, head_part = second_step(
            operands[0], operands[1], all_live, gain_second, second_in, second_out, head_weight
        )
        return ((running[0] + in_part, running[1] + out_part, running[2] + head_part), grad_one)

    weight_sums, work_grad_stack = lax.scan(
        worker_block, (zero_in, zero_out, head_sum), (work_pair_stack, work_target_stack)
    )
    work_grads = work_grad_stack.reshape(work_count, tile_len, width)
    back_rank = col_count * slot_iota + jnp.mod(col_index - offsets[:, None], col_count)
    back_valid = back_rank < row_counts[:, None]
    back_position = jnp.minimum((offsets[:, None] + back_rank) // col_count, work_count - 1)
    back_pairs = jnp.where(
        back_valid[:, :, None, None], work_grads[back_position], jnp.zeros((), jnp.bfloat16)
    )
    returned = lax.all_to_all(back_pairs, "col", split_axis=0, concat_axis=0, tiled=True)
    tile_worker = jnp.mod(my_offset + rank_of, col_count)
    tile_slot = jnp.minimum(rank_of // col_count, slots - 1)
    from_worker = returned.reshape(col_count * slots, tile_len, width)[
        tile_worker * slots + tile_slot
    ]
    grad_one_all = jnp.where(tile_live[:, None, None], from_worker, rest_tiles).reshape(
        rows_dev * cols_dev, width
    )
    grad_one_stack = grad_one_all.reshape(row_blocks, block_pairs, width)

    def backward_block(running, operands):
        block_index, grad_one = operands
        start_z = start_field(block_index)
        unused_delta, saved = transition_forward(start_z, gain_first, first_in, first_out)
        back_field, unused_in, unused_out = transition_backward(
            saved, grad_one, gain_first, first_in, first_out, False
        )
        grad_zero = (grad_one.astype(jnp.float32) + back_field).reshape(block_rows, cols_dev, width)
        return (
            running + jnp.sum(grad_zero, axis=0),
            (grad_zero.astype(jnp.bfloat16), jnp.sum(grad_zero, axis=1)),
        )

    right_grad, (pair_grad_stack, left_stack) = lax.scan(
        backward_block, jnp.zeros((cols_dev, width), jnp.float32), (block_ids, grad_one_stack)
    )
    pair_grad = pair_grad_stack.reshape(rows_dev, cols_dev, width)
    left_grad = left_stack.reshape(rows_dev, width)
    token_part = jnp.zeros((token_count, 2 * width), jnp.float32)
    token_part = lax.dynamic_update_slice(token_part, left_grad, (row_index * rows_dev, 0))
    token_part = lax.dynamic_update_slice(token_part, right_grad, (col_start, width))
    token_total, in_total, out_total, head_total = lax.psum(
        (token_part, weight_sums[0], weight_sums[1], weight_sums[2]), ("row", "col")
    )
    token_rows = lax.dynamic_slice_in_dim(token_total, row_index * rows_dev, rows_dev, 0).astype(
        jnp.bfloat16
    )
    single_grad = contract(token_rows, proj_weight, 1, 1)
    return (
        pair_grad,
        single_grad,
        in_total / token_count,
        out_total / token_count,
        head_total / token_count,
    )


def solution(mesh):
    in_specs = (
        P("row", "col"),
        P("row", "col", None),
        P("col", None),
        P(),
        P(),
        P(),
        P(),
        P(),
        P(),
        P(),
        P("row", "col"),
        P(),
        P("row", None),
        P("row", "col"),
    )
    out_specs = (P("row", "col", None), P("row", "col"), P(), P(), P())
    return jax.shard_map(local, mesh=mesh, in_specs=in_specs, out_specs=out_specs, check_vma=False)
```

profile of v0, /device:TPU:1, one launch (start us, length us, event | category | flops | bytes accessed | tf_op | source)
XLA Modules:
  0.0 618.8 jit_solution(7770418198475508663)
XLA Ops:
  7.9 1.5 fusion.87
  13.8 1.9 gather_fusion.2
  21.9 7.6 %all-to-all-start.1 = ((bf16[16,2,256]{2,1,0:T(2,128)(2,1)}), bf16[16,2,256]{2,1,0:T(2,128)(2,1)S(1)}, u32[]{:S(2)}, u32[]{:S(2)}) async-start(bf16[16,2,256]{2,1,0:T(2,128)(2,1)} %reshape.938), calls=%async_computation.1 | async-start | bytes 32768 | tf_op jit(solution)/shard_map/all_to_all | solution.py:187
  30.6 10.0 %fusion.77 = s32[128]{0:T(128)S(1)} fusion(s32[128]{0:T(128)S(1)} %convert_reduce_fusion.1, s32[]{:T(128)} %bitcast.33, s32[]{:T(128)} %bitcast.34, s32[]{:T(128)} %bitcast.35, s32[]{:T(128)} %bitcast.36, s32[]{:T(128)} %bitcast.37, s32[]{:T(128)} %bitcast.39, s32[]{:T(128)} %bitcast.38, s32[]{:T(128)} %bitcast.16, s32[]{:T(128)} %bitcast.18, s32[]{:T(128)} %bitcast.20, ...), kind=kLoop, calls=%fused_computation.208 | loop fusion | flops 7296 | bytes 1092 | tf_op jit(solution)/shard_map/select_n | solution.py:195
  42.0 54.0 %all-reduce.6.cloned.1.call-done = f32[128,256]{1,0:T(8,128)} async-done(((f32[128,256]{1,0:T(8,128)}), f32[128,256]{1,0:T(8,128)}) %all-reduce.6.cloned.1.call-update) | async-done | bytes 131088 | tf_op jit(solution)/shard_map/psum | solution.py:114
  96.8 15.6 %all_gather.3 = bf16[1024,128]{1,0:T(8,128)(2,1)S(1)} all-gather(bf16[128,128]{1,0:T(8,128)(2,1)S(1)} %slice.95), channel_id=1, replica_groups=mesh['row'=8,'col'=16] {'row'}, dimensions={0}, use_global_device_ids=true | all-gather | bytes 294912 | tf_op jit(solution)/shard_map/all_gather | solution.py:118
  112.5 1.5 slice.72
  113.9 1.6 broadcast.784.clone
  115.5 64.0 %while.55 = (s32[]{:T(128)}, bf16[8,1024,128]{2,1,0:T(8,128)(2,1)}, s32[8]{0:T(128)S(1)}, bf16[128,64,128]{2,1,0:T(8,128)(2,1)}, f32[128,128]{1,0:T(8,128)}, /*i...) while((s32[]{:T(128)}, bf16[8,1024,128]{2,1,0:T(8,128)(2,1)}, ...), condition=%wide.region_6.7_spmd, body=%wide.region_3.6_spmd.sunk | while | flops 407897088 | bytes 11818179 | solution.py:138
  118.7 1.4 multiply_reduce_fusion.5
  121.2 2.3 fusion.163
  126.7 1.4 multiply_reduce_fusion.5
  129.2 2.3 fusion.163
  134.7 1.4 multiply_reduce_fusion.5
  137.2 2.3 fusion.163
  142.7 1.4 multiply_reduce_fusion.5
  145.2 2.3 fusion.163
  153.2 2.3 fusion.163
  158.7 1.4 multiply_reduce_fusion.5
  161.2 2.3 fusion.163
  166.7 1.4 multiply_reduce_fusion.5
  169.2 2.3 fusion.163
  177.2 2.3 fusion.163
  179.6 2.6 gather_fusion.3
  182.2 1.6 broadcast_select_fusion
  183.7 4.8 all-to-all-start
  189.2 22.2 %while.56 = (s32[]{:T(128)}, f32[128,64]{0,1:T(8,128)S(1)}, bf16[8,1024,128]{2,1,0:T(8,128)(2,1)S(1)}, bf16[8,1024,128]{2,1,0:T(8,128)(2,1)}, bf16[128,64]{0,1:T...) while((s32[]{:T(128)}, f32[128,64]{0,1:T(8,128)S(1)}, ...), condition=%wide.region_10.11_spmd.clone, body=%wide.region_7.10_spmd.clone.sunk | while | flops 51592192 | bytes 1995891 | solution.py:166
  211.5 9.9 %all-to-all-done = bf16[16,16,32,128]{3,2,1,0:T(8,128)(2,1)} async-done(((bf16[16,16,32,128]{3,2,1,0:T(8,128)(2,1)}), bf16[16,16,32,128]{3,2,1,0:T(8,128)(2,1)}, u32[]{:S(2)}, u32[]{:S(2)}) %all-to-all-start) | async-done | bytes 2097184 | tf_op jit(solution)/shard_map/all_to_all | solution.py:186
  221.4 2.4 gather_fusion.4
  223.8 45.5 %while.57 = (s32[]{:T(128)}, f32[128,1024]{1,0:T(8,128)}, f32[512,128]{1,0:T(8,128)S(1)}, f32[128,64]{0,1:T(8,128)S(1)}, bf16[4,1024,128]{2,1,0:T(8,128)(2,1)}, ...) while((s32[]{:T(128)}, f32[128,1024]{1,0:T(8,128)}, ...), condition=%wide.region_19.20_spmd.clone, body=%wide.region_12.19_spmd.clone.sunk | while | flops 1282874368 | bytes 39037144 | solution.py:209
  231.5 3.5 fusion.189
  242.8 3.7 fusion.189
  254.2 3.7 fusion.189
  265.6 3.7 fusion.189
  269.3 2.3 gather_fusion.7
  271.6 1.5 broadcast_select_fusion.1
  273.2 3.7 all-to-all-start.2
  278.3 161.1 %all-reduce.8.cloned.1.call-done = (f32[128,1024]{1,0:T(8,128)}, f32[512,128]{1,0:T(8,128)}) async-done(((f32[128,1024]{1,0:T(8,128)}, f32[512,128]{1,0:T(8,128)}), (f32[128,1024]{1,0:T(8,128)}, f32[512,128]{1,0:T(8,128)})) %all-reduce.8.cloned.1.call-update) | async-done | bytes 786448 | tf_op jit(solution)/shard_map/psum | solution.py:251
  439.5 1.7 broadcast_multiply_fusion.8
  441.1 1.9 broadcast_multiply_fusion.7
  443.0 2.2 gather_fusion.8
  445.2 3.6 bitcast_select_fusion
  448.7 89.8 %while.58 = (s32[]{:T(128)}, f32[64,128]{1,0:T(8,128)S(1)}, bf16[8,16,64,128]{3,2,1,0:T(8,128)(2,1)}, f32[8,16,128]{2,1,0:T(8,128)}, bf16[8,1024,128]{2,1,0:T(8,...) while((s32[]{:T(128)}, f32[64,128]{1,0:T(8,128)S(1)}, ...), condition=%wide.region_27.28_spmd.clone, body=%wide.region_20.27_spmd.clone.sunk | while | flops 686169088 | bytes 20674808 | solution.py:243
  454.5 2.0 fusion.198
  456.5 1.4 fusion.199
  465.7 2.0 fusion.198
  467.8 1.4 fusion.199
  474.3 1.4 multiply_reduce_fusion.6
  476.9 2.0 fusion.198
  479.0 1.4 fusion.199
  485.5 1.4 multiply_reduce_fusion.6
  488.2 2.0 fusion.198
  490.2 1.4 fusion.199
  499.4 2.0 fusion.198
  501.4 1.4 fusion.199
  508.0 1.4 multiply_reduce_fusion.6
  510.6 2.0 fusion.198
  512.7 1.4 fusion.199
  521.8 2.0 fusion.198
  523.9 1.4 fusion.199
  530.4 1.4 multiply_reduce_fusion.6
  533.0 2.0 fusion.198
  535.1 1.4 fusion.199
  539.5 71.1 %all-reduce.9 = (bf16[1024,256]{1,0:T(8,128)(2,1)S(1)}, f32[128,64]{0,1:T(8,128)S(1)}) all-reduce(f32[1024,256]{1,0:T(8,128)S(1)} %constant_dynamic-update-slice_fusion.2, f32[128,64]{0,1:T(8,128)S(1)} %get-tuple-element.223), channel_id=1, replica_groups=mesh['row'=8,'col'=16] {'row','col'}, use_global_device_ids=true, to_apply=%region_28.29 | all-reduce | flops 270336 | bytes 1638400 | tf_op jit(solution)/shard_map/psum | solution.py:251
  (440 shorter events, 153.7 us)
Async XLA Ops:
  7.2 0.7 copy-start
  7.2 6.6 %copy-start.1 = (s32[1,256]{1,0:T(1,128)S(1)}, s32[1,256]{1,0:T(1,128)}, u32[]{:S(2)}) copy-start(s32[1,256]{1,0:T(1,128)} %param.35) | copy-start | bytes 3076
  7.2 88.8 %all-reduce.6.cloned.1.call-start = ((), (), s32[]{:S(2)}) async-start(), calls=%async_computation.3 | async-start | bytes 262144 | tf_op jit(solution)/shard_map/psum | solution.py:114
  13.8 3.7 copy-start.9
  13.8 5.6 copy-start.11
  20.2 95.3 %copy-start.2 = (bf16[128,1024]{1,0:T(8,128)(2,1)S(1)}, bf16[128,1024]{1,0:T(8,128)(2,1)}, u32[]{:S(2)}) copy-start(bf16[128,1024]{1,0:T(8,128)(2,1)} %param.26) | copy-start | bytes 786436
  20.2 95.3 %copy-start.8 = (f32[128]{0:T(128)S(1)}, f32[128]{0:T(128)}, u32[]{:S(2)}) copy-start(f32[128]{0:T(128)} %param.25) | copy-start | bytes 1540
  21.9 19.1 %all-to-all-start.1 = ((bf16[16,2,256]{2,1,0:T(2,128)(2,1)}), bf16[16,2,256]{2,1,0:T(2,128)(2,1)S(1)}, u32[]{:S(2)}, u32[]{:S(2)}) async-start(bf16[16,2,256]{2,1,0:T(2,128)(2,1)} %reshape.938), calls=%async_computation.1 | async-start | bytes 32768 | tf_op jit(solution)/shard_map/all_to_all | solution.py:187
  183.7 37.7 %all-to-all-start = ((bf16[16,16,32,128]{3,2,1,0:T(8,128)(2,1)}), bf16[16,16,32,128]{3,2,1,0:T(8,128)(2,1)}, u32[]{:S(2)}, u32[]{:S(2)}) async-start(bf16[16,16,32,128]{3,2,1,0:T(8,128)(2,1)} %broadcast_select_fusion), calls=%async_computation | async-start | bytes 4194304 | tf_op jit(solution)/shard_map/all_to_all | solution.py:186
  188.5 0.7 copy-start.7
  211.4 10.0 %copy-start.4 = (bf16[8,1024,128]{2,1,0:T(8,128)(2,1)}, bf16[8,1024,128]{2,1,0:T(8,128)(2,1)S(1)}, u32[]{:S(2)}) copy-start(bf16[8,1024,128]{2,1,0:T(8,128)(2,1)S(1)} %get-tuple-element.217) | copy-start | bytes 6291460
  211.4 12.3 %copy-start.5 = (bf16[128,1024]{1,0:T(8,128)(2,1)S(1)}, bf16[128,1024]{1,0:T(8,128)(2,1)}, u32[]{:S(2)}) copy-start(bf16[128,1024]{1,0:T(8,128)(2,1)} %param.29) | copy-start | bytes 786436
  211.4 12.3 %copy-start.6 = (bf16[512,128]{1,0:T(8,128)(2,1)S(1)}, bf16[512,128]{1,0:T(8,128)(2,1)}, u32[]{:S(2)}) copy-start(bf16[512,128]{1,0:T(8,128)(2,1)} %param.30) | copy-start | bytes 393220
  211.4 12.3 %copy-start.10 = (f32[128]{0:T(128)S(1)}, f32[128]{0:T(128)}, u32[]{:S(2)}) copy-start(f32[128]{0:T(128)} %param.28) | copy-start | bytes 1540
  228.1 1.4 copy-start.12
  228.1 1.4 copy-start.13
  239.4 1.4 copy-start.12
  239.4 1.4 copy-start.13
  250.8 1.4 copy-start.12
  250.8 1.4 copy-start.13
  262.2 1.4 copy-start.12
  262.2 1.4 copy-start.13
  269.3 2.3 copy-start.3
  273.2 169.8 %all-to-all-start.2 = ((bf16[16,16,32,128]{3,2,1,0:T(8,128)(2,1)}), bf16[16,16,32,128]{3,2,1,0:T(8,128)(2,1)S(1)}, u32[]{:S(2)}, u32[]{:S(2)}) async-start(bf16[16,16,32,128]{3,2,1,0:T(8,128)(2,1)} %broadcast_select_fusion.1), calls=%async_computation.2 | async-start | bytes 4194304 | tf_op jit(solution)/shard_map/all_to_all | solution.py:219
  276.9 162.6 %all-reduce.8.cloned.1.call-start = ((), (), s32[]{:S(2)}) async-start(), calls=%async_computation.4 | async-start | bytes 1572864 | tf_op jit(solution)/shard_map/psum | solution.py:251
Sparse Core Ops, SparseCore 0:
  11.8 84.1 all-reduce.5
  283.0 156.3 all-reduce.7
where the time goes:
time: 623 us; the launch traced here: 619 us
  waiting for transfers between devices  226 us (36%)
  matrix products  115 us (18%)
  other arithmetic  88.6 us (14%)
  blocking collectives  86.8 us (14%)
  local copies, waits for them, and re-layouts  58.9 us (9%)
  starting transfers between devices  16.4 us (3%)
  between operations  14.5 us (2%)
  loops' own time  12.6 us (2%)
    psum x1, waiting for transfers between devices, local(): lax.psum((token_part, weight_sums[0], weight_sums[1], weight_sums[2]), ('...  161 us
    psum x1, blocking collectives, local(): lax.psum((token_part, weight_sums[0], weight_sums[1], weight_sums[2]), ('...  71.1 us
    dot_general x57, matrix products, contract(): lax.dot_general(left_op, right_op, (((left_dim,), (right_dim,)), ((), ())...  68 us
    psum x1, waiting for transfers between devices, local(): projected = lax.psum(partial_proj, 'col')  54 us
    reduce_sum x20, other arithmetic, transition_forward(): jnp.mean(centred * centred, axis=-1, keepdims=True) + 1e-05  23.1 us
    dot_general x12, matrix products, transition_forward(): result = jnp.dot(hidden_act, w_out, preferred_element_type=jnp.float32)  20.6 us
    reduce_sum x20, other arithmetic, transition_forward(): average = jnp.mean(start_z, axis=-1, keepdims=True)  19.2 us
    all_gather x1, blocking collectives, local(): right_all = lax.all_gather(right_part, 'row', axis=0, tiled=True)  15.6 us
  transfers between devices with their start and end apart: 5, of which 3 were waited for; matrix products, arithmetic and copies ran while one was open for 8% of the time, Pallas kernels for 0%

commit v1 on v0

--- a/solution.py
+++ b/solution.py
@@ -249,7 +249,7 @@
     token_part = lax.dynamic_update_slice(token_part, left_grad, (row_index * rows_dev, 0))
     token_part = lax.dynamic_update_slice(token_part, right_grad, (col_start, width))
     token_total, in_total, out_total, head_total = lax.psum(
-        (token_part, weight_sums[0], weight_sums[1], weight_sums[2]), ("row", "col")
+        lax.psum((token_part, weight_sums[0], weight_sums[1], weight_sums[2]), "col"), "row"
     )
     token_rows = lax.dynamic_slice_in_dim(token_total, row_index * rows_dev, rows_dev, 0).astype(
         jnp.bfloat16

time: 623 us -> 571 us (0.917)
  waiting for transfers between devices: 226 us -> 133 us
  blocking collectives: 86.8 us -> 126 us
    psum x1 -> x2, waiting for transfers between devices: 161 us -> 39.8 us  [the longest x1 30.5 us: local(): lax.psum((token_part, weight_sums[0], weight_sums[1], weight_sums[2]), 'c...]
    psum x1 -> x2, blocking collectives: 71.1 us -> 110 us  [the longest x1 56.7 us: local(): lax.psum((token_part, weight_sums[0], weight_sums[1], weight_sums[2]), 'c...]
    all_to_all x1, waiting for transfers between devices: 0.01 us -> 28.7 us  [local(): lax.all_to_all(back_pairs, 'col', split_axis=0, concat_axis=0, tiled=True)]
  transfers between devices with their start and end apart: 5 -> 6, of which waited for: 3 -> 5; matrix products, arithmetic and copies ran while one was open for 8% -> 9% of each run, Pallas kernels for 0% -> 0%
where the time goes in v1:
time: 571 us; the launch traced here: 566 us
  waiting for transfers between devices  133 us (23%)
  blocking collectives  126 us (22%)
  matrix products  116 us (20%)
  other arithmetic  88.6 us (16%)
  local copies, waits for them, and re-layouts  60 us (11%)
  starting transfers between devices  16.4 us (3%)
  between operations  14.2 us (2%)
  loops' own time  12.6 us (2%)
    dot_general x57, matrix products, contract(): lax.dot_general(left_op, right_op, (((left_dim,), (right_dim,)), ((), ())...  68 us
    psum x1, blocking collectives, local(): lax.psum((token_part, weight_sums[0], weight_sums[1], weight_sums[2]), 'c...  56.7 us
    psum x1, waiting for transfers between devices, local(): projected = lax.psum(partial_proj, 'col')  54 us
    psum x1, blocking collectives, local(): lax.psum(lax.psum((token_part, weight_sums[0], weight_sums[1], weight_sum...  53.4 us
    psum x1, waiting for transfers between devices, local(): lax.psum((token_part, weight_sums[0], weight_sums[1], weight_sums[2]), 'c...  30.5 us
    all_to_all x1, waiting for transfers between devices, local(): lax.all_to_all(back_pairs, 'col', split_axis=0, concat_axis=0, tiled=True)  28.7 us
    reduce_sum x20, other arithmetic, transition_forward(): jnp.mean(centred * centred, axis=-1, keepdims=True) + 1e-05  23.1 us
    dot_general x12, matrix products, transition_forward(): result = jnp.dot(hidden_act, w_out, preferred_element_type=jnp.float32)  20.6 us
  transfers between devices with their start and end apart: 6, of which 5 were waited for; matrix products, arithmetic and copies ran while one was open for 9% of the time, Pallas kernels for 0%

profile of v1, /device:TPU:1, one launch (start us, length us, event | category | flops | bytes accessed | tf_op | source)
XLA Modules:
  0.0 565.6 jit_solution(16017105605605874845)
XLA Ops:
  7.9 1.5 fusion.87
  13.8 1.9 gather_fusion.2
  21.9 7.6 %all-to-all-start.1 = ((bf16[16,2,256]{2,1,0:T(2,128)(2,1)}), bf16[16,2,256]{2,1,0:T(2,128)(2,1)S(1)}, u32[]{:S(2)}, u32[]{:S(2)}) async-start(bf16[16,2,256]{2,1,0:T(2,128)(2,1)} %reshape.938), calls=%async_computation.1 | async-start | bytes 32768 | tf_op jit(solution)/shard_map/all_to_all | solution.py:187
  30.6 10.0 %fusion.77 = s32[128]{0:T(128)S(1)} fusion(s32[128]{0:T(128)S(1)} %convert_reduce_fusion.1, s32[]{:T(128)} %bitcast.33, s32[]{:T(128)} %bitcast.34, s32[]{:T(128)} %bitcast.35, s32[]{:T(128)} %bitcast.36, s32[]{:T(128)} %bitcast.37, s32[]{:T(128)} %bitcast.39, s32[]{:T(128)} %bitcast.38, s32[]{:T(128)} %bitcast.16, s32[]{:T(128)} %bitcast.18, s32[]{:T(128)} %bitcast.20, ...), kind=kLoop, calls=%fused_computation.208 | loop fusion | flops 7296 | bytes 1092 | tf_op jit(solution)/shard_map/select_n | solution.py:195
  42.0 54.0 %all-reduce.8.cloned.1.call-done = f32[128,256]{1,0:T(8,128)} async-done(((f32[128,256]{1,0:T(8,128)}), f32[128,256]{1,0:T(8,128)}) %all-reduce.8.cloned.1.call-update) | async-done | bytes 131088 | tf_op jit(solution)/shard_map/psum | solution.py:114
  96.8 15.6 %all_gather.3 = bf16[1024,128]{1,0:T(8,128)(2,1)S(1)} all-gather(bf16[128,128]{1,0:T(8,128)(2,1)S(1)} %slice.95), channel_id=1, replica_groups=mesh['row'=8,'col'=16] {'row'}, dimensions={0}, use_global_device_ids=true | all-gather | bytes 294912 | tf_op jit(solution)/shard_map/all_gather | solution.py:118
  112.5 1.5 slice.72
  113.9 1.6 broadcast.784.clone
  115.5 64.0 %while.55 = (s32[]{:T(128)}, bf16[8,1024,128]{2,1,0:T(8,128)(2,1)}, s32[8]{0:T(128)S(1)}, bf16[128,64,128]{2,1,0:T(8,128)(2,1)}, f32[128,128]{1,0:T(8,128)}, /*i...) while((s32[]{:T(128)}, bf16[8,1024,128]{2,1,0:T(8,128)(2,1)}, ...), condition=%wide.region_6.7_spmd, body=%wide.region_3.6_spmd.sunk | while | flops 407897088 | bytes 11818179 | solution.py:138
  121.2 2.3 fusion.163
  126.7 1.4 multiply_reduce_fusion.5
  129.2 2.3 fusion.163
  137.2 2.3 fusion.163
  142.7 1.4 multiply_reduce_fusion.5
  145.2 2.3 fusion.163
  153.2 2.3 fusion.163
  158.7 1.4 multiply_reduce_fusion.5
  161.2 2.3 fusion.163
  166.7 1.4 multiply_reduce_fusion.5
  169.2 2.3 fusion.163
  177.2 2.3 fusion.163
  179.6 2.6 gather_fusion.3
  182.2 1.6 broadcast_select_fusion
  183.7 4.8 all-to-all-start
  189.2 22.2 %while.56 = (s32[]{:T(128)}, f32[128,64]{0,1:T(8,128)S(1)}, bf16[8,1024,128]{2,1,0:T(8,128)(2,1)S(1)}, bf16[8,1024,128]{2,1,0:T(8,128)(2,1)}, bf16[128,64]{0,1:T...) while((s32[]{:T(128)}, f32[128,64]{0,1:T(8,128)S(1)}, ...), condition=%wide.region_10.11_spmd.clone, body=%wide.region_7.10_spmd.clone.sunk | while | flops 51592192 | bytes 1995891 | solution.py:166
  211.5 9.9 %all-to-all-done = bf16[16,16,32,128]{3,2,1,0:T(8,128)(2,1)} async-done(((bf16[16,16,32,128]{3,2,1,0:T(8,128)(2,1)}), bf16[16,16,32,128]{3,2,1,0:T(8,128)(2,1)}, u32[]{:S(2)}, u32[]{:S(2)}) %all-to-all-start) | async-done | bytes 2097184 | tf_op jit(solution)/shard_map/all_to_all | solution.py:186
  221.4 2.4 gather_fusion.4
  223.8 45.5 %while.57 = (s32[]{:T(128)}, f32[128,1024]{1,0:T(8,128)}, f32[512,128]{1,0:T(8,128)S(1)}, f32[128,64]{0,1:T(8,128)S(1)}, bf16[4,1024,128]{2,1,0:T(8,128)(2,1)}, ...) while((s32[]{:T(128)}, f32[128,1024]{1,0:T(8,128)}, ...), condition=%wide.region_19.20_spmd.clone, body=%wide.region_12.19_spmd.clone.sunk | while | flops 1282874368 | bytes 39037144 | solution.py:209
  231.5 3.5 fusion.189
  242.8 3.7 fusion.189
  254.2 3.7 fusion.189
  265.6 3.7 fusion.189
  269.3 2.3 gather_fusion.7
  271.6 1.5 broadcast_select_fusion.1
  273.2 3.7 all-to-all-start.2
  277.9 28.7 %all-to-all-done.2 = bf16[16,16,32,128]{3,2,1,0:T(8,128)(2,1)S(1)} async-done(((bf16[16,16,32,128]{3,2,1,0:T(8,128)(2,1)}), bf16[16,16,32,128]{3,2,1,0:T(8,128)(2,1)S(1)}, u32[]{:S(2)}, u32[]{:S(2)}) %all-to-all-start.2) | async-done | bytes 2097184 | tf_op jit(solution)/shard_map/all_to_all | solution.py:219
  306.6 2.2 gather_fusion.8
  308.7 3.6 bitcast_select_fusion
  312.3 89.8 %while.58 = (s32[]{:T(128)}, f32[64,128]{1,0:T(8,128)S(1)}, bf16[8,16,64,128]{3,2,1,0:T(8,128)(2,1)}, f32[8,16,128]{2,1,0:T(8,128)}, bf16[8,1024,128]{2,1,0:T(8,...) while((s32[]{:T(128)}, f32[64,128]{1,0:T(8,128)S(1)}, ...), condition=%wide.region_27.28_spmd.clone, body=%wide.region_20.27_spmd.clone.sunk | while | flops 686169088 | bytes 20674808 | solution.py:243
  318.1 2.0 fusion.198
  320.1 1.4 fusion.199
  329.3 2.0 fusion.198
  331.3 1.4 fusion.199
  340.5 2.0 fusion.198
  342.5 1.4 fusion.199
  351.7 2.0 fusion.198
  353.8 1.4 fusion.199
  360.3 1.4 multiply_reduce_fusion.6
  362.9 2.0 fusion.198
  365.0 1.4 fusion.199
  374.2 2.0 fusion.198
  376.2 1.4 fusion.199
  382.8 1.4 multiply_reduce_fusion.6
  385.4 2.0 fusion.198
  387.4 1.4 fusion.199
  394.0 1.4 multiply_reduce_fusion.6
  396.6 2.0 fusion.198
  398.7 1.4 fusion.199
  404.1 56.7 %psum.70 = f32[128,64]{0,1:T(8,128)S(1)} all-reduce(f32[128,64]{0,1:T(8,128)S(1)} %get-tuple-element.223), channel_id=1, replica_groups=mesh['row'=8,'col'=16] {'col'}, use_global_device_ids=true, to_apply=%region_34.35 | all-reduce | flops 8192 | bytes 65536 | tf_op jit(solution)/shard_map/psum | solution.py:252
  460.8 30.5 %all-reduce.10.cloned.1.call-done = (f32[1024,256]{1,0:T(8,128)}, f32[128,1024]{1,0:T(8,128)}, f32[512,128]{1,0:T(8,128)}) async-done(((f32[1024,256]{1,0:T(8,128)}, f32[128,1024]{1,0:T(8,128)}, f32[512,128]{1,0:T(8,128)}), (f32[1024,256]{1,0:T(8,128)}, f32[128,1024]{1,0:T(8,128)}, f32[512,128]{1,0:T(8,128)})) %all-reduce.10.cloned.1.call-update) | async-done | bytes 1835024 | tf_op jit(solution)/shard_map/psum | solution.py:252
  491.3 53.4 %all-reduce.13 = (bf16[1024,256]{1,0:T(8,128)(2,1)S(1)}, f32[128,64]{0,1:T(8,128)S(1)}) all-reduce(f32[1024,256]{1,0:T(8,128)} %get-tuple-element.405, f32[128,64]{0,1:T(8,128)S(1)} %psum.70), channel_id=1, replica_groups=mesh['row'=8,'col'=16] {'row'}, use_global_device_ids=true, to_apply=%region_29.30 | all-reduce | flops 270336 | bytes 1638400 | tf_op jit(solution)/shard_map/psum | solution.py:251
  546.1 9.4 %all-reduce.12.cloned.1.call-done = (f32[128,1024]{1,0:T(8,128)}, f32[512,128]{1,0:T(8,128)}) async-done(((f32[128,1024]{1,0:T(8,128)}, f32[512,128]{1,0:T(8,128)}), (f32[128,1024]{1,0:T(8,128)}, f32[512,128]{1,0:T(8,128)})) %all-reduce.12.cloned.1.call-update) | async-done | bytes 786448 | tf_op jit(solution)/shard_map/psum | solution.py:251
  555.5 1.9 broadcast_multiply_fusion.7
  557.4 1.7 broadcast_multiply_fusion.8
  (446 shorter events, 158.4 us)
Async XLA Ops:
  7.2 0.7 copy-start
  7.2 6.6 %copy-start.1 = (s32[1,256]{1,0:T(1,128)S(1)}, s32[1,256]{1,0:T(1,128)}, u32[]{:S(2)}) copy-start(s32[1,256]{1,0:T(1,128)} %param.35) | copy-start | bytes 3076
  7.2 88.8 %all-reduce.8.cloned.1.call-start = ((), (), s32[]{:S(2)}) async-start(), calls=%async_computation.3 | async-start | bytes 262144 | tf_op jit(solution)/shard_map/psum | solution.py:114
  13.8 3.7 copy-start.10
  13.8 5.6 copy-start.12
  20.2 95.3 %copy-start.2 = (bf16[128,1024]{1,0:T(8,128)(2,1)S(1)}, bf16[128,1024]{1,0:T(8,128)(2,1)}, u32[]{:S(2)}) copy-start(bf16[128,1024]{1,0:T(8,128)(2,1)} %param.26) | copy-start | bytes 786436
  20.2 95.3 %copy-start.9 = (f32[128]{0:T(128)S(1)}, f32[128]{0:T(128)}, u32[]{:S(2)}) copy-start(f32[128]{0:T(128)} %param.25) | copy-start | bytes 1540
  21.9 19.1 %all-to-all-start.1 = ((bf16[16,2,256]{2,1,0:T(2,128)(2,1)}), bf16[16,2,256]{2,1,0:T(2,128)(2,1)S(1)}, u32[]{:S(2)}, u32[]{:S(2)}) async-start(bf16[16,2,256]{2,1,0:T(2,128)(2,1)} %reshape.938), calls=%async_computation.1 | async-start | bytes 32768 | tf_op jit(solution)/shard_map/all_to_all | solution.py:187
  183.7 37.6 %all-to-all-start = ((bf16[16,16,32,128]{3,2,1,0:T(8,128)(2,1)}), bf16[16,16,32,128]{3,2,1,0:T(8,128)(2,1)}, u32[]{:S(2)}, u32[]{:S(2)}) async-start(bf16[16,16,32,128]{3,2,1,0:T(8,128)(2,1)} %broadcast_select_fusion), calls=%async_computation | async-start | bytes 4194304 | tf_op jit(solution)/shard_map/all_to_all | solution.py:186
  188.5 0.7 copy-start.8
  211.4 9.9 %copy-start.4 = (bf16[8,1024,128]{2,1,0:T(8,128)(2,1)}, bf16[8,1024,128]{2,1,0:T(8,128)(2,1)S(1)}, u32[]{:S(2)}) copy-start(bf16[8,1024,128]{2,1,0:T(8,128)(2,1)S(1)} %get-tuple-element.217) | copy-start | bytes 6291460
  211.4 12.3 %copy-start.5 = (bf16[128,1024]{1,0:T(8,128)(2,1)S(1)}, bf16[128,1024]{1,0:T(8,128)(2,1)}, u32[]{:S(2)}) copy-start(bf16[128,1024]{1,0:T(8,128)(2,1)} %param.29) | copy-start | bytes 786436
  211.5 12.3 %copy-start.7 = (bf16[512,128]{1,0:T(8,128)(2,1)S(1)}, bf16[512,128]{1,0:T(8,128)(2,1)}, u32[]{:S(2)}) copy-start(bf16[512,128]{1,0:T(8,128)(2,1)} %param.30) | copy-start | bytes 393220
  211.5 12.3 %copy-start.11 = (f32[128]{0:T(128)S(1)}, f32[128]{0:T(128)}, u32[]{:S(2)}) copy-start(f32[128]{0:T(128)} %param.28) | copy-start | bytes 1540
  228.1 1.4 copy-start.13
  228.1 1.4 copy-start.14
  239.4 1.4 copy-start.13
  239.4 1.4 copy-start.14
  250.8 1.4 copy-start.13
  250.8 1.4 copy-start.14
  262.2 1.4 copy-start.13
  262.2 1.4 copy-start.14
  269.3 2.3 copy-start.3
  273.2 33.4 %all-to-all-start.2 = ((bf16[16,16,32,128]{3,2,1,0:T(8,128)(2,1)}), bf16[16,16,32,128]{3,2,1,0:T(8,128)(2,1)S(1)}, u32[]{:S(2)}, u32[]{:S(2)}) async-start(bf16[16,16,32,128]{3,2,1,0:T(8,128)(2,1)} %broadcast_select_fusion.1), calls=%async_computation.2 | async-start | bytes 4194304 | tf_op jit(solution)/shard_map/all_to_all | solution.py:219
  276.9 214.4 %all-reduce.10.cloned.1.call-start = ((), (), s32[]{:S(2)}) async-start(), calls=%async_computation.4 | async-start | bytes 3670016 | tf_op jit(solution)/shard_map/psum | solution.py:252
  403.0 1.0 copy-start.6
  404.1 151.4 %all-reduce.12.cloned.1.call-start = ((), (), s32[]{:S(2)}) async-start(), calls=%async_computation.5 | async-start | bytes 1572864 | tf_op jit(solution)/shard_map/psum | solution.py:251
Sparse Core Ops, SparseCore 0:
  11.8 84.1 all-reduce.7
  404.2 87.0 all-reduce.9
  493.7 61.6 all-reduce.11
